TPU v7x, 32 devices: a whole 2x2x4 slice. The times are simulated.
32 devices in a mesh: dp: 2 (over x), pipe: 4 (over z), mp: 4 (over y, core).
Axes of the slice: x: 2, y: 2, z: 4, core: 2. Of those that a mesh axis runs over, the one named last changes fastest.
Arguments:
- inputs: bfloat16 [4, 128, 1024], P(None, 'dp', 'mp'), may hold values from -6 to 6
- cotangent: bfloat16 [4, 128, 1024], P(None, 'dp', 'mp'), may hold values from -6 to 6
- gain: float32 [4, 1024], P('pipe'), may hold values from 0.25 to 1.75
- weight_in: bfloat16 [4, 1024, 32768], P('pipe', None, 'mp'), may hold values from -0.1875 to 0.1875
- weight_out: bfloat16 [4, 32768, 1024], P('pipe', 'mp'), may hold values from -0.03125 to 0.03125
Outputs:
- grad_in: bfloat16 [4, 1024, 32768], P('pipe', 'dp', 'mp')
- grad_out: bfloat16 [4, 32768, 1024], P('pipe', 'mp', 'dp')
- grad_gain: float32 [4, 1024], P('pipe', 'mp')
All inputs are finite; a program needn't handle non-finite values.
Results may differ from a plain program's by a relative error of at most 0.023.
Values may be sent and summed in bfloat16 or wider, within the bound.
A program may use at most 128 MiB of HBM per device.

v0:
```python
import math
import jax
import jax.numpy as jnp
from jax import lax
from jax.sharding import PartitionSpec as P

GELU_COEF = math.sqrt(2.0 / math.pi)
CUBIC_COEF = 0.044715
NORM_EPS = 1e-06
CONTRACT_LAST = (((1,), (1,)), ((), ()))
CONTRACT_FIRST = (((0,), (0,)), ((), ()))


def shifted(shard, axis, by):
    count = lax.axis_size(axis)
    pairs = [(i, i + by) for i in range(count) if 0 <= i + by < count]
    return lax.ppermute(shard, axis, pairs)


def gelu_parts(values):
    tangent = jnp.tanh(GELU_COEF * (values + CUBIC_COEF * values * values * values))
    output = 0.5 * values * (1.0 + tangent)
    derivative = 0.5 * (1.0 + tangent) + 0.5 * values * (1.0 - tangent * tangent) * GELU_COEF * (
        1.0 + 3.0 * CUBIC_COEF * values * values
    )
    return (output, derivative)


def shards(inputs, cotangent, gain, weight_in, weight_out):
    segment_count = lax.axis_size("pipe")
    section = lax.axis_index("pipe")
    part_index = lax.axis_index("mp")
    replicas = lax.axis_size("dp")
    micro, row_count, width = inputs.shape
    weight_first = weight_in[0]
    weight_second = weight_out[0]
    gain_row = gain[0]
    full_width = gain_row.shape[0]
    hidden = weight_first.shape[1]
    gain_own = lax.dynamic_slice_in_dim(gain_row, part_index * width, width, 0)
    turns = segment_count + micro - 1

    def forward_turn(turn, carry):
        incoming, rows_save, scale_save, gate_save = carry
        micro_slot = turn - section
        is_active = (micro_slot >= 0) & (micro_slot < micro)
        slot_index = jnp.clip(micro_slot, 0, micro - 1)
        first_rows = lax.dynamic_index_in_dim(inputs, slot_index, 0, keepdims=False)
        segment_input = jnp.where(section == 0, first_rows, incoming)
        whole_rows = lax.all_gather(segment_input, "mp", axis=1, tiled=True)

        def forward_active(operands):
            gathered, rows_keep, scale_keep, gate_keep = operands
            values = gathered.astype(jnp.float32)
            inv_rms = lax.rsqrt(jnp.mean(values * values, axis=1) + NORM_EPS)
            normed = (values * inv_rms[:, None] * gain_row).astype(jnp.bfloat16)
            gate_input = jnp.dot(normed, weight_first, preferred_element_type=jnp.float32)
            activated = gelu_parts(gate_input)[0].astype(jnp.bfloat16)
            branch = jnp.dot(activated, weight_second, preferred_element_type=jnp.float32)
            rows_keep = lax.dynamic_update_index_in_dim(rows_keep, gathered, slot_index, 0)
            scale_keep = lax.dynamic_update_index_in_dim(scale_keep, inv_rms, slot_index, 0)
            gate_keep = lax.dynamic_update_index_in_dim(gate_keep, gate_input, slot_index, 0)
            return (branch, rows_keep, scale_keep, gate_keep)

        def forward_resting(operands):
            gathered, rows_keep, scale_keep, gate_keep = operands
            return (
                jnp.zeros((row_count, full_width), jnp.float32),
                rows_keep,
                scale_keep,
                gate_keep,
            )

        branch, rows_save, scale_save, gate_save = lax.cond(
            is_active,
            forward_active,
            forward_resting,
            (whole_rows, rows_save, scale_save, gate_save),
        )
        branch_sum = lax.psum_scatter(branch, "mp", scatter_dimension=1, tiled=True)
        result = (segment_input.astype(jnp.float32) + branch_sum).astype(jnp.bfloat16)
        passed = shifted(result, "pipe", 1)
        return (passed, rows_save, scale_save, gate_save)

    forward_init = (
        jnp.zeros((row_count, width), jnp.bfloat16),
        jnp.zeros((micro, row_count, full_width), jnp.bfloat16),
        jnp.zeros((micro, row_count), jnp.float32),
        jnp.zeros((micro, row_count, hidden), jnp.float32),
    )
    forward_out = lax.fori_loop(0, turns, forward_turn, forward_init)
    rows_save = forward_out[1]
    scale_save = forward_out[2]
    gate_save = forward_out[3]

    def backward_turn(turn, carry):
        incoming, pregrad_save, outgrad_save, gain_acc = carry
        micro_slot = turn - (segment_count - 1 - section)
        is_active = (micro_slot >= 0) & (micro_slot < micro)
        slot_index = jnp.clip(micro_slot, 0, micro - 1)
        last_rows = lax.dynamic_index_in_dim(cotangent, slot_index, 0, keepdims=False).astype(
            jnp.float32
        )
        grad_rows = jnp.where(section == segment_count - 1, last_rows, incoming)
        whole_grad = lax.all_gather(grad_rows.astype(jnp.bfloat16), "mp", axis=1, tiled=True)

        def backward_active(operands):
            gathered, pregrad_keep, outgrad_keep = operands
            gate_input = lax.dynamic_index_in_dim(gate_save, slot_index, 0, keepdims=False)
            slopes = gelu_parts(gate_input)[1]
            inner_grad = lax.dot_general(
                gathered, weight_second, CONTRACT_LAST, preferred_element_type=jnp.float32
            )
            pre_grad = (inner_grad * slopes).astype(jnp.bfloat16)
            norm_part = lax.dot_general(
                pre_grad, weight_first, CONTRACT_LAST, preferred_element_type=jnp.float32
            )
            pregrad_keep = lax.dynamic_update_index_in_dim(pregrad_keep, pre_grad, slot_index, 0)
            outgrad_keep = lax.dynamic_update_index_in_dim(outgrad_keep, gathered, slot_index, 0)
            return (norm_part, pregrad_keep, outgrad_keep)

        def backward_resting(operands):
            gathered, pregrad_keep, outgrad_keep = operands
            return (jnp.zeros((row_count, full_width), jnp.float32), pregrad_keep, outgrad_keep)

        norm_part, pregrad_save, outgrad_save = lax.cond(
            is_active, backward_active, backward_resting, (whole_grad, pregrad_save, outgrad_save)
        )
        values = lax.dynamic_index_in_dim(rows_save, slot_index, 0, keepdims=False).astype(
            jnp.float32
        )
        inv_rms = lax.dynamic_index_in_dim(scale_save, slot_index, 0, keepdims=False)
        unit_full = values * inv_rms[:, None]
        unit_own = lax.dynamic_slice_in_dim(unit_full, part_index * width, width, 1)
        norm_grad = lax.psum_scatter(norm_part, "mp", scatter_dimension=1, tiled=True)
        scaled = norm_grad * gain_own
        row_dot = lax.psum(jnp.sum(scaled * unit_own, axis=1), "mp")
        previous = grad_rows + inv_rms[:, None] * (
            scaled - unit_own * row_dot[:, None] / full_width
        )
        gain_acc = gain_acc + jnp.where(is_active, jnp.sum(norm_grad * unit_own, axis=0), 0.0)
        passed = shifted(previous, "pipe", -1)
        return (passed, pregrad_save, outgrad_save, gain_acc)

    backward_init = (
        jnp.zeros((row_count, width), jnp.float32),
        jnp.zeros((micro, row_count, hidden), jnp.bfloat16),
        jnp.zeros((micro, row_count, full_width), jnp.bfloat16),
        jnp.zeros((width,), jnp.float32),
    )
    backward_out = lax.fori_loop(0, turns, backward_turn, backward_init)
    all_rows = micro * row_count
    pregrad_all = backward_out[1].reshape(all_rows, hidden)
    outgrad_all = backward_out[2].reshape(all_rows, full_width)
    gain_acc = backward_out[3]
    normed_all = (
        (rows_save.astype(jnp.float32) * scale_save[:, :, None] * gain_row)
        .astype(jnp.bfloat16)
        .reshape(all_rows, full_width)
    )
    activated_all = gelu_parts(gate_save)[0].astype(jnp.bfloat16).reshape(all_rows, hidden)
    half_width = full_width // replicas
    packed = jnp.stack((normed_all, outgrad_all)).reshape(2, all_rows, replicas, half_width)
    swapped = lax.all_to_all(packed, "dp", split_axis=2, concat_axis=1, tiled=True)
    columns = swapped.reshape(2, replicas * all_rows, half_width)
    pregrad_piece = lax.all_gather(pregrad_all, "dp", axis=0, tiled=True)
    activated_piece = lax.all_gather(activated_all, "dp", axis=0, tiled=True)
    normed_cols = columns[0]
    outgrad_cols = columns[1]
    in_term = lax.dot_general(
        normed_cols, pregrad_piece, CONTRACT_FIRST, preferred_element_type=jnp.float32
    )
    out_term = lax.dot_general(
        outgrad_cols, activated_piece, CONTRACT_FIRST, preferred_element_type=jnp.float32
    )
    grad_sums = jnp.stack((in_term, out_term))
    in_part = grad_sums[0]
    out_part = grad_sums[1]
    grad_first = in_part.astype(jnp.bfloat16)[None]
    grad_second = out_part.astype(jnp.bfloat16).T[None]
    gain_total = lax.psum(gain_acc, "dp")[None]
    return (grad_first, grad_second, gain_total)


def solution(mesh):
    in_specs = (
        P(None, "dp", "mp"),
        P(None, "dp", "mp"),
        P("pipe", None),
        P("pipe", None, "mp"),
        P("pipe", "mp", None),
    )
    out_specs = (P("pipe", "dp", "mp"), P("pipe", "mp", "dp"), P("pipe", "mp"))
    return jax.shard_map(shards, mesh=mesh, in_specs=in_specs, out_specs=out_specs, check_vma=False)
```

profile of v0, /device:TPU:0, one launch (start us, length us, event | category | flops | bytes accessed | tf_op | source)
XLA Modules:
  0.0 1032.1 jit_solution(17084897989914273569)
XLA Ops:
  13.2 334.4 %while.42 = (s32[]{:T(128)}, bf16[64,256]{1,0:T(8,128)(2,1)S(1)}, bf16[4,64,1024]{2,1,0:T(8,128)(2,1)S(1)}, f32[4,64]{1,0:T(4,128)S(1)}, f32[4,64,8192]{2,1,0:T(...) while((s32[]{:T(128)}, bf16[64,256]{1,0:T(8,128)(2,1)S(1)}, ...), condition=%wide.region_5.6_spmd, body=%wide.region_0.5_spmd.sunk | while | flops 2152726528 | bytes 110303480 | solution.py:91
  14.0 6.5 all_gather.28
  20.5 14.5 %conditional.5 = (f32[64,1024]{1,0:T(8,128)S(1)}, bf16[4,64,1024]{2,1,0:T(8,128)(2,1)S(1)}, f32[4,64]{1,0:T(4,128)S(1)}, f32[4,64,8192]{2,1,0:T(8,128)}) conditional(s32[]{:T(128)} %convert_element_type.141, (bf16[4,64,1024]{2,1,0:T(8,128)(2,1)S(1)}, f32[4,64]{1,0:T(4,128)S(1)}, f32[4,64,8192]{2,1,0:T(8,128)}) %tuple.97, ...), branch_computations={%region_1.1_spmd, %region_2.3_spmd} | conditional | flops 2152660992 | bytes 107747168 | solution.py:74
  20.7 10.4 %bitcast_dynamic-update-slice_fusion = (f32[4,64,8192]{2,1,0:T(8,128)}, f32[64,8192]{1,0:T(8,128)S(1)}) fusion(f32[4,64,8192]{2,1,0:T(8,128)} %get-tuple-element.578, s32[]{:T(128)S(6)} %select_n.85, bf16[1024,8192]{1,0:T(8,128)(2,1)} %get-tuple-element.573, bf16[64,1024]{1,0:T(8,128)(2,1)S(1)} %get-tuple-element.571, f32[1024]{0:T(1024)S(1)} %bitcast.78, ...), kind=kOutput, calls=%fused_computation.6 | convolution fusion | flops 1074003968 | bytes 21106948 | tf_op jit(solution)/shard_map/while/body/eval_jaxpr/cond/branch_1_fun/dot_general | solution.py:57
  35.8 18.8 %reduce-scatter.3.cloned.1.call-done = f32[64,256]{1,0:T(8,128)} async-done(((f32[64,1024]{1,0:T(8,128)}), f32[64,256]{1,0:T(8,128)}) %reduce-scatter.3.cloned.1.call-update) | async-done | bytes 65552 | tf_op jit(solution)/shard_map/while/body/eval_jaxpr/reduce_scatter | solution.py:80
  61.2 5.4 all_gather.28
  66.6 14.5 %conditional.5 = (f32[64,1024]{1,0:T(8,128)S(1)}, bf16[4,64,1024]{2,1,0:T(8,128)(2,1)S(1)}, f32[4,64]{1,0:T(4,128)S(1)}, f32[4,64,8192]{2,1,0:T(8,128)}) conditional(s32[]{:T(128)} %convert_element_type.141, (bf16[4,64,1024]{2,1,0:T(8,128)(2,1)S(1)}, f32[4,64]{1,0:T(4,128)S(1)}, f32[4,64,8192]{2,1,0:T(8,128)}) %tuple.97, ...), branch_computations={%region_1.1_spmd, %region_2.3_spmd} | conditional | flops 2152660992 | bytes 107747168 | solution.py:74
  66.7 10.4 %bitcast_dynamic-update-slice_fusion = (f32[4,64,8192]{2,1,0:T(8,128)}, f32[64,8192]{1,0:T(8,128)S(1)}) fusion(f32[4,64,8192]{2,1,0:T(8,128)} %get-tuple-element.578, s32[]{:T(128)S(6)} %select_n.85, bf16[1024,8192]{1,0:T(8,128)(2,1)} %get-tuple-element.573, bf16[64,1024]{1,0:T(8,128)(2,1)S(1)} %get-tuple-element.571, f32[1024]{0:T(1024)S(1)} %bitcast.78, ...), kind=kOutput, calls=%fused_computation.6 | convolution fusion | flops 1074003968 | bytes 21106948 | tf_op jit(solution)/shard_map/while/body/eval_jaxpr/cond/branch_1_fun/dot_general | solution.py:57
  81.9 19.2 %reduce-scatter.3.cloned.1.call-done = f32[64,256]{1,0:T(8,128)} async-done(((f32[64,1024]{1,0:T(8,128)}), f32[64,256]{1,0:T(8,128)}) %reduce-scatter.3.cloned.1.call-update) | async-done | bytes 65552 | tf_op jit(solution)/shard_map/while/body/eval_jaxpr/reduce_scatter | solution.py:80
  107.7 5.4 all_gather.28
  113.1 14.5 %conditional.5 = (f32[64,1024]{1,0:T(8,128)S(1)}, bf16[4,64,1024]{2,1,0:T(8,128)(2,1)S(1)}, f32[4,64]{1,0:T(4,128)S(1)}, f32[4,64,8192]{2,1,0:T(8,128)}) conditional(s32[]{:T(128)} %convert_element_type.141, (bf16[4,64,1024]{2,1,0:T(8,128)(2,1)S(1)}, f32[4,64]{1,0:T(4,128)S(1)}, f32[4,64,8192]{2,1,0:T(8,128)}) %tuple.97, ...), branch_computations={%region_1.1_spmd, %region_2.3_spmd} | conditional | flops 2152660992 | bytes 107747168 | solution.py:74
  113.2 10.4 %bitcast_dynamic-update-slice_fusion = (f32[4,64,8192]{2,1,0:T(8,128)}, f32[64,8192]{1,0:T(8,128)S(1)}) fusion(f32[4,64,8192]{2,1,0:T(8,128)} %get-tuple-element.578, s32[]{:T(128)S(6)} %select_n.85, bf16[1024,8192]{1,0:T(8,128)(2,1)} %get-tuple-element.573, bf16[64,1024]{1,0:T(8,128)(2,1)S(1)} %get-tuple-element.571, f32[1024]{0:T(1024)S(1)} %bitcast.78, ...), kind=kOutput, calls=%fused_computation.6 | convolution fusion | flops 1074003968 | bytes 21106948 | tf_op jit(solution)/shard_map/while/body/eval_jaxpr/cond/branch_1_fun/dot_general | solution.py:57
  128.4 20.1 %reduce-scatter.3.cloned.1.call-done = f32[64,256]{1,0:T(8,128)} async-done(((f32[64,1024]{1,0:T(8,128)}), f32[64,256]{1,0:T(8,128)}) %reduce-scatter.3.cloned.1.call-update) | async-done | bytes 65552 | tf_op jit(solution)/shard_map/while/body/eval_jaxpr/reduce_scatter | solution.py:80
  155.1 5.4 all_gather.28
  160.5 14.6 %conditional.5 = (f32[64,1024]{1,0:T(8,128)S(1)}, bf16[4,64,1024]{2,1,0:T(8,128)(2,1)S(1)}, f32[4,64]{1,0:T(4,128)S(1)}, f32[4,64,8192]{2,1,0:T(8,128)}) conditional(s32[]{:T(128)} %convert_element_type.141, (bf16[4,64,1024]{2,1,0:T(8,128)(2,1)S(1)}, f32[4,64]{1,0:T(4,128)S(1)}, f32[4,64,8192]{2,1,0:T(8,128)}) %tuple.97, ...), branch_computations={%region_1.1_spmd, %region_2.3_spmd} | conditional | flops 2152660992 | bytes 107747168 | solution.py:74
  160.6 10.3 %bitcast_dynamic-update-slice_fusion = (f32[4,64,8192]{2,1,0:T(8,128)}, f32[64,8192]{1,0:T(8,128)S(1)}) fusion(f32[4,64,8192]{2,1,0:T(8,128)} %get-tuple-element.578, s32[]{:T(128)S(6)} %select_n.85, bf16[1024,8192]{1,0:T(8,128)(2,1)} %get-tuple-element.573, bf16[64,1024]{1,0:T(8,128)(2,1)S(1)} %get-tuple-element.571, f32[1024]{0:T(1024)S(1)} %bitcast.78, ...), kind=kOutput, calls=%fused_computation.6 | convolution fusion | flops 1074003968 | bytes 21106948 | tf_op jit(solution)/shard_map/while/body/eval_jaxpr/cond/branch_1_fun/dot_general | solution.py:57
  175.8 21.0 %reduce-scatter.3.cloned.1.call-done = f32[64,256]{1,0:T(8,128)} async-done(((f32[64,1024]{1,0:T(8,128)}), f32[64,256]{1,0:T(8,128)}) %reduce-scatter.3.cloned.1.call-update) | async-done | bytes 65552 | tf_op jit(solution)/shard_map/while/body/eval_jaxpr/reduce_scatter | solution.py:80
  203.4 5.4 all_gather.28
  209.6 35.6 %reduce-scatter.3.cloned.1.call-done = f32[64,256]{1,0:T(8,128)} async-done(((f32[64,1024]{1,0:T(8,128)}), f32[64,256]{1,0:T(8,128)}) %reduce-scatter.3.cloned.1.call-update) | async-done | bytes 65552 | tf_op jit(solution)/shard_map/while/body/eval_jaxpr/reduce_scatter | solution.py:80
  251.7 5.4 all_gather.28
  257.9 35.6 %reduce-scatter.3.cloned.1.call-done = f32[64,256]{1,0:T(8,128)} async-done(((f32[64,1024]{1,0:T(8,128)}), f32[64,256]{1,0:T(8,128)}) %reduce-scatter.3.cloned.1.call-update) | async-done | bytes 65552 | tf_op jit(solution)/shard_map/while/body/eval_jaxpr/reduce_scatter | solution.py:80
  300.0 5.4 all_gather.28
  306.2 35.6 %reduce-scatter.3.cloned.1.call-done = f32[64,256]{1,0:T(8,128)} async-done(((f32[64,1024]{1,0:T(8,128)}), f32[64,256]{1,0:T(8,128)}) %reduce-scatter.3.cloned.1.call-update) | async-done | bytes 65552 | tf_op jit(solution)/shard_map/while/body/eval_jaxpr/reduce_scatter | solution.py:80
  347.6 6.1 fusion.48
  356.2 443.4 %while.43 = (s32[]{:T(128)}, f32[64,256]{1,0:T(8,128)S(1)}, bf16[4,64,8192]{2,1,0:T(8,128)(2,1)}, bf16[4,64,1024]{2,1,0:T(8,128)(2,1)S(1)}, f32[256]{0:T(256)S(1...) while((s32[]{:T(128)}, f32[64,256]{1,0:T(8,128)S(1)}, ...), condition=%wide.region_13.14_spmd.clone, body=%wide.region_6.13_spmd.clone.sunk | while | flops 2157756928 | bytes 42672648 | solution.py:151
  356.5 5.4 all_gather.29
  362.7 44.6 %reduce-scatter.5.cloned.1.call-done = f32[64,256]{1,0:T(8,128)} async-done(((f32[64,1024]{1,0:T(8,128)}), f32[64,256]{1,0:T(8,128)}) %reduce-scatter.5.cloned.1.call-update) | async-done | bytes 65552 | tf_op jit(solution)/shard_map/while/body/eval_jaxpr/reduce_scatter | solution.py:135
  408.4 5.8 psum.23
  416.4 4.8 collective-permute-done.1
  421.2 5.4 all_gather.29
  427.5 43.4 %reduce-scatter.5.cloned.1.call-done = f32[64,256]{1,0:T(8,128)} async-done(((f32[64,1024]{1,0:T(8,128)}), f32[64,256]{1,0:T(8,128)}) %reduce-scatter.5.cloned.1.call-update) | async-done | bytes 65552 | tf_op jit(solution)/shard_map/while/body/eval_jaxpr/reduce_scatter | solution.py:135
  471.9 5.8 psum.23
  484.8 5.4 all_gather.29
  491.0 43.4 %reduce-scatter.5.cloned.1.call-done = f32[64,256]{1,0:T(8,128)} async-done(((f32[64,1024]{1,0:T(8,128)}), f32[64,256]{1,0:T(8,128)}) %reduce-scatter.5.cloned.1.call-update) | async-done | bytes 65552 | tf_op jit(solution)/shard_map/while/body/eval_jaxpr/reduce_scatter | solution.py:135
  535.4 5.8 psum.23
  548.3 5.4 all_gather.29
  553.7 23.6 %conditional.6 = (f32[64,1024]{1,0:T(8,128)S(1)}, bf16[4,64,8192]{2,1,0:T(8,128)(2,1)}, bf16[4,64,1024]{2,1,0:T(8,128)(2,1)S(1)}) conditional(s32[]{:T(128)} %convert_element_type.142, (bf16[4,64,8192]{2,1,0:T(8,128)(2,1)}, bf16[4,64,1024]{2,1,0:T(8,128)(2,1)S(1)}) %tuple.101, (bf16[64,1024]{1,0:T(8,128)(2,1)S(1)}, bf16[8192,1024]{1,0:T(8,128)(2,1)}, ...), branch_computations={%region_7.7_spmd, %region_8.8_spmd} | conditional | flops 2157445120 | bytes 39452740 | solution.py:126
  553.7 12.6 %bitcast_dynamic-update-slice_fusion.2 = (bf16[4,64,8192]{2,1,0:T(8,128)(2,1)}, bf16[64,8192]{1,0:T(8,128)(2,1)S(1)}) fusion(bf16[4,64,8192]{2,1,0:T(8,128)(2,1)} %get-tuple-element.602, s32[]{:T(128)S(6)} %select_n.88, f32[4,64,8192]{2,1,0:T(8,128)} %get-tuple-element.599, bf16[64,1024]{1,0:T(8,128)(2,1)S(1)} %get-tuple-element.597, ...), kind=kOutput, calls=%fused_computation.41 | convolution fusion | flops 1083703296 | bytes 21102596 | tf_op jit(solution)/shard_map/while/body/eval_jaxpr/cond/branch_1_fun/dot_general | solution.py:111
  566.4 11.0 %fusion.50 = f32[64,1024]{1,0:T(8,128)S(1)} fusion(bf16[64,8192]{1,0:T(8,128)(2,1)S(1)} %get-tuple-element.748, bf16[1024,8192]{1,0:T(8,128)(2,1)} %get-tuple-element.601), kind=kOutput, calls=%fused_computation.74 | convolution fusion | flops 1073741824 | bytes 18087936 | tf_op jit(solution)/shard_map/while/body/eval_jaxpr/cond/branch_1_fun/dot_general | solution.py:115
  578.1 19.8 %reduce-scatter.5.cloned.1.call-done = f32[64,256]{1,0:T(8,128)} async-done(((f32[64,1024]{1,0:T(8,128)}), f32[64,256]{1,0:T(8,128)}) %reduce-scatter.5.cloned.1.call-update) | async-done | bytes 65552 | tf_op jit(solution)/shard_map/while/body/eval_jaxpr/reduce_scatter | solution.py:135
  598.9 5.8 psum.23
  611.8 5.4 all_gather.29
  617.2 23.6 %conditional.6 = (f32[64,1024]{1,0:T(8,128)S(1)}, bf16[4,64,8192]{2,1,0:T(8,128)(2,1)}, bf16[4,64,1024]{2,1,0:T(8,128)(2,1)S(1)}) conditional(s32[]{:T(128)} %convert_element_type.142, (bf16[4,64,8192]{2,1,0:T(8,128)(2,1)}, bf16[4,64,1024]{2,1,0:T(8,128)(2,1)S(1)}) %tuple.101, (bf16[64,1024]{1,0:T(8,128)(2,1)S(1)}, bf16[8192,1024]{1,0:T(8,128)(2,1)}, ...), branch_computations={%region_7.7_spmd, %region_8.8_spmd} | conditional | flops 2157445120 | bytes 39452740 | solution.py:126
  617.2 12.6 %bitcast_dynamic-update-slice_fusion.2 = (bf16[4,64,8192]{2,1,0:T(8,128)(2,1)}, bf16[64,8192]{1,0:T(8,128)(2,1)S(1)}) fusion(bf16[4,64,8192]{2,1,0:T(8,128)(2,1)} %get-tuple-element.602, s32[]{:T(128)S(6)} %select_n.88, f32[4,64,8192]{2,1,0:T(8,128)} %get-tuple-element.599, bf16[64,1024]{1,0:T(8,128)(2,1)S(1)} %get-tuple-element.597, ...), kind=kOutput, calls=%fused_computation.41 | convolution fusion | flops 1083703296 | bytes 21102596 | tf_op jit(solution)/shard_map/while/body/eval_jaxpr/cond/branch_1_fun/dot_general | solution.py:111
  629.9 10.9 %fusion.50 = f32[64,1024]{1,0:T(8,128)S(1)} fusion(bf16[64,8192]{1,0:T(8,128)(2,1)S(1)} %get-tuple-element.748, bf16[1024,8192]{1,0:T(8,128)(2,1)} %get-tuple-element.601), kind=kOutput, calls=%fused_computation.74 | convolution fusion | flops 1073741824 | bytes 18087936 | tf_op jit(solution)/shard_map/while/body/eval_jaxpr/cond/branch_1_fun/dot_general | solution.py:115
  641.6 19.8 %reduce-scatter.5.cloned.1.call-done = f32[64,256]{1,0:T(8,128)} async-done(((f32[64,1024]{1,0:T(8,128)}), f32[64,256]{1,0:T(8,128)}) %reduce-scatter.5.cloned.1.call-update) | async-done | bytes 65552 | tf_op jit(solution)/shard_map/while/body/eval_jaxpr/reduce_scatter | solution.py:135
  662.5 5.8 psum.23
  675.4 5.4 all_gather.29
  680.8 23.6 %conditional.6 = (f32[64,1024]{1,0:T(8,128)S(1)}, bf16[4,64,8192]{2,1,0:T(8,128)(2,1)}, bf16[4,64,1024]{2,1,0:T(8,128)(2,1)S(1)}) conditional(s32[]{:T(128)} %convert_element_type.142, (bf16[4,64,8192]{2,1,0:T(8,128)(2,1)}, bf16[4,64,1024]{2,1,0:T(8,128)(2,1)S(1)}) %tuple.101, (bf16[64,1024]{1,0:T(8,128)(2,1)S(1)}, bf16[8192,1024]{1,0:T(8,128)(2,1)}, ...), branch_computations={%region_7.7_spmd, %region_8.8_spmd} | conditional | flops 2157445120 | bytes 39452740 | solution.py:126
  680.8 12.6 %bitcast_dynamic-update-slice_fusion.2 = (bf16[4,64,8192]{2,1,0:T(8,128)(2,1)}, bf16[64,8192]{1,0:T(8,128)(2,1)S(1)}) fusion(bf16[4,64,8192]{2,1,0:T(8,128)(2,1)} %get-tuple-element.602, s32[]{:T(128)S(6)} %select_n.88, f32[4,64,8192]{2,1,0:T(8,128)} %get-tuple-element.599, bf16[64,1024]{1,0:T(8,128)(2,1)S(1)} %get-tuple-element.597, ...), kind=kOutput, calls=%fused_computation.41 | convolution fusion | flops 1083703296 | bytes 21102596 | tf_op jit(solution)/shard_map/while/body/eval_jaxpr/cond/branch_1_fun/dot_general | solution.py:111
  693.4 11.0 %fusion.50 = f32[64,1024]{1,0:T(8,128)S(1)} fusion(bf16[64,8192]{1,0:T(8,128)(2,1)S(1)} %get-tuple-element.748, bf16[1024,8192]{1,0:T(8,128)(2,1)} %get-tuple-element.601), kind=kOutput, calls=%fused_computation.74 | convolution fusion | flops 1073741824 | bytes 18087936 | tf_op jit(solution)/shard_map/while/body/eval_jaxpr/cond/branch_1_fun/dot_general | solution.py:115
  705.2 18.9 %reduce-scatter.5.cloned.1.call-done = f32[64,256]{1,0:T(8,128)} async-done(((f32[64,1024]{1,0:T(8,128)}), f32[64,256]{1,0:T(8,128)}) %reduce-scatter.5.cloned.1.call-update) | async-done | bytes 65552 | tf_op jit(solution)/shard_map/while/body/eval_jaxpr/reduce_scatter | solution.py:135
  725.1 5.8 psum.23
  738.0 5.4 all_gather.29
  743.4 23.6 %conditional.6 = (f32[64,1024]{1,0:T(8,128)S(1)}, bf16[4,64,8192]{2,1,0:T(8,128)(2,1)}, bf16[4,64,1024]{2,1,0:T(8,128)(2,1)S(1)}) conditional(s32[]{:T(128)} %convert_element_type.142, (bf16[4,64,8192]{2,1,0:T(8,128)(2,1)}, bf16[4,64,1024]{2,1,0:T(8,128)(2,1)S(1)}) %tuple.101, (bf16[64,1024]{1,0:T(8,128)(2,1)S(1)}, bf16[8192,1024]{1,0:T(8,128)(2,1)}, ...), branch_computations={%region_7.7_spmd, %region_8.8_spmd} | conditional | flops 2157445120 | bytes 39452740 | solution.py:126
  743.4 12.6 %bitcast_dynamic-update-slice_fusion.2 = (bf16[4,64,8192]{2,1,0:T(8,128)(2,1)}, bf16[64,8192]{1,0:T(8,128)(2,1)S(1)}) fusion(bf16[4,64,8192]{2,1,0:T(8,128)(2,1)} %get-tuple-element.602, s32[]{:T(128)S(6)} %select_n.88, f32[4,64,8192]{2,1,0:T(8,128)} %get-tuple-element.599, bf16[64,1024]{1,0:T(8,128)(2,1)S(1)} %get-tuple-element.597, ...), kind=kOutput, calls=%fused_computation.41 | convolution fusion | flops 1083703296 | bytes 21102596 | tf_op jit(solution)/shard_map/while/body/eval_jaxpr/cond/branch_1_fun/dot_general | solution.py:111
  756.0 11.0 %fusion.50 = f32[64,1024]{1,0:T(8,128)S(1)} fusion(bf16[64,8192]{1,0:T(8,128)(2,1)S(1)} %get-tuple-element.748, bf16[1024,8192]{1,0:T(8,128)(2,1)} %get-tuple-element.601), kind=kOutput, calls=%fused_computation.74 | convolution fusion | flops 1073741824 | bytes 18087936 | tf_op jit(solution)/shard_map/while/body/eval_jaxpr/cond/branch_1_fun/dot_general | solution.py:115
  767.8 18.0 %reduce-scatter.5.cloned.1.call-done = f32[64,256]{1,0:T(8,128)} async-done(((f32[64,1024]{1,0:T(8,128)}), f32[64,256]{1,0:T(8,128)}) %reduce-scatter.5.cloned.1.call-update) | async-done | bytes 65552 | tf_op jit(solution)/shard_map/while/body/eval_jaxpr/reduce_scatter | solution.py:135
  786.8 5.8 psum.23
  808.0 21.2 %psum.20 = f32[1,256]{1,0:T(1,128)} all-reduce(f32[1,256]{1,0:T(1,128)S(1)} %bitcast.82), channel_id=1, replica_groups=mesh['dp'=2,'pipe'=4,'mp'=4] {'dp'}, use_global_device_ids=true, to_apply=%region_14.15 | all-reduce | flops 256 | bytes 2048 | tf_op jit(solution)/shard_map/psum | solution.py:181
  829.4 81.4 %all-gather.5.cloned.1.call-done = bf16[512,8192]{1,0:T(8,128)(2,1)} async-done(((bf16[256,8192]{1,0:T(8,128)(2,1)}), bf16[512,8192]{1,0:T(8,128)(2,1)}) %all-gather.5.cloned.1.call-update) | async-done | bytes 8388624 | tf_op jit(solution)/shard_map/all_gather | solution.py:167
  910.8 10.5 %fusion.43 = bf16[1,8192,512]{2,1,0:T(8,128)(2,1)} fusion(bf16[512,8192]{1,0:T(8,128)(2,1)} %all-gather.5.cloned.1.call-done, bf16[512,512]{1,0:T(8,128)(2,1)S(1)} %bitcast.80), kind=kOutput, calls=%fused_computation.63 | convolution fusion | flops 4299161600 | bytes 17301504 | tf_op jit(solution)/shard_map/dot_general | solution.py:173
  921.3 93.5 %all-gather.3.cloned.1.call-done = bf16[512,8192]{1,0:T(8,128)(2,1)} async-done(((bf16[256,8192]{1,0:T(8,128)(2,1)}), bf16[512,8192]{1,0:T(8,128)(2,1)}) %all-gather.3.cloned.1.call-update) | async-done | bytes 8388624 | tf_op jit(solution)/shard_map/all_gather | solution.py:166
  1014.8 10.2 fusion.42
  (209 shorter events, 141.4 us)
Async XLA Ops:
  8.7 4.5 copy-start.3
  13.2 41.4 %reduce-scatter.3.cloned.1.call-start = ((), (), s32[]{:S(2)}) async-start(), calls=%async_computation.5 | async-start | bytes 327680 | tf_op jit(solution)/shard_map/while/body/eval_jaxpr/reduce_scatter | solution.py:80
  20.7 11.3 %copy-start = (bf16[8192,1024]{1,0:T(8,128)(2,1)S(1)}, bf16[8192,1024]{1,0:T(8,128)(2,1)}, u32[]{:S(2)}) copy-start(bf16[8192,1024]{1,0:T(8,128)(2,1)} %get-tuple-element.574) | copy-start | bytes 50331652 | tf_op jit(solution)/shard_map/while/body/eval_jaxpr/cond
  35.1 0.7 copy-start.1
  55.5 5.0 collective-permute-start
  60.4 40.7 %reduce-scatter.3.cloned.1.call-start = ((), (), s32[]{:S(2)}) async-start(), calls=%async_computation.5 | async-start | bytes 327680 | tf_op jit(solution)/shard_map/while/body/eval_jaxpr/reduce_scatter | solution.py:80
  66.7 11.3 %copy-start = (bf16[8192,1024]{1,0:T(8,128)(2,1)S(1)}, bf16[8192,1024]{1,0:T(8,128)(2,1)}, u32[]{:S(2)}) copy-start(bf16[8192,1024]{1,0:T(8,128)(2,1)} %get-tuple-element.574) | copy-start | bytes 50331652 | tf_op jit(solution)/shard_map/while/body/eval_jaxpr/cond
  81.1 0.7 copy-start.1
  102.0 5.0 collective-permute-start
  106.9 41.6 %reduce-scatter.3.cloned.1.call-start = ((), (), s32[]{:S(2)}) async-start(), calls=%async_computation.5 | async-start | bytes 327680 | tf_op jit(solution)/shard_map/while/body/eval_jaxpr/reduce_scatter | solution.py:80
  113.2 11.3 %copy-start = (bf16[8192,1024]{1,0:T(8,128)(2,1)S(1)}, bf16[8192,1024]{1,0:T(8,128)(2,1)}, u32[]{:S(2)}) copy-start(bf16[8192,1024]{1,0:T(8,128)(2,1)} %get-tuple-element.574) | copy-start | bytes 50331652 | tf_op jit(solution)/shard_map/while/body/eval_jaxpr/cond
  127.6 0.7 copy-start.1
  149.3 5.0 collective-permute-start
  154.3 42.5 %reduce-scatter.3.cloned.1.call-start = ((), (), s32[]{:S(2)}) async-start(), calls=%async_computation.5 | async-start | bytes 327680 | tf_op jit(solution)/shard_map/while/body/eval_jaxpr/reduce_scatter | solution.py:80
  160.6 11.3 %copy-start = (bf16[8192,1024]{1,0:T(8,128)(2,1)S(1)}, bf16[8192,1024]{1,0:T(8,128)(2,1)}, u32[]{:S(2)}) copy-start(bf16[8192,1024]{1,0:T(8,128)(2,1)} %get-tuple-element.574) | copy-start | bytes 50331652 | tf_op jit(solution)/shard_map/while/body/eval_jaxpr/cond
  175.0 0.7 copy-start.1
  197.7 5.0 collective-permute-start
  202.6 42.5 %reduce-scatter.3.cloned.1.call-start = ((), (), s32[]{:S(2)}) async-start(), calls=%async_computation.5 | async-start | bytes 327680 | tf_op jit(solution)/shard_map/while/body/eval_jaxpr/reduce_scatter | solution.py:80
  208.9 0.7 copy-start.1
  246.0 5.0 collective-permute-start
  251.0 42.5 %reduce-scatter.3.cloned.1.call-start = ((), (), s32[]{:S(2)}) async-start(), calls=%async_computation.5 | async-start | bytes 327680 | tf_op jit(solution)/shard_map/while/body/eval_jaxpr/reduce_scatter | solution.py:80
  257.2 0.7 copy-start.1
  294.3 5.0 collective-permute-start
  299.3 42.5 %reduce-scatter.3.cloned.1.call-start = ((), (), s32[]{:S(2)}) async-start(), calls=%async_computation.5 | async-start | bytes 327680 | tf_op jit(solution)/shard_map/while/body/eval_jaxpr/reduce_scatter | solution.py:80
  305.5 0.7 copy-start.1
  342.6 5.0 collective-permute-start
  353.7 2.6 copy-start.4
  356.4 50.9 %reduce-scatter.5.cloned.1.call-start = ((), (), s32[]{:S(2)}) async-start(), calls=%async_computation.6 | async-start | bytes 327680 | tf_op jit(solution)/shard_map/while/body/eval_jaxpr/reduce_scatter | solution.py:135
  362.0 0.7 copy-start.2
  415.1 6.2 collective-permute-start.1
  421.2 49.7 %reduce-scatter.5.cloned.1.call-start = ((), (), s32[]{:S(2)}) async-start(), calls=%async_computation.6 | async-start | bytes 327680 | tf_op jit(solution)/shard_map/while/body/eval_jaxpr/reduce_scatter | solution.py:135
  426.7 0.7 copy-start.2
  478.6 6.2 collective-permute-start.1
  484.8 49.6 %reduce-scatter.5.cloned.1.call-start = ((), (), s32[]{:S(2)}) async-start(), calls=%async_computation.6 | async-start | bytes 327680 | tf_op jit(solution)/shard_map/while/body/eval_jaxpr/reduce_scatter | solution.py:135
  490.2 0.7 copy-start.2
  542.1 6.2 collective-permute-start.1
  548.3 49.6 %reduce-scatter.5.cloned.1.call-start = ((), (), s32[]{:S(2)}) async-start(), calls=%async_computation.6 | async-start | bytes 327680 | tf_op jit(solution)/shard_map/while/body/eval_jaxpr/reduce_scatter | solution.py:135
  577.3 0.7 copy-start.2
  605.6 6.2 collective-permute-start.1
  611.8 49.7 %reduce-scatter.5.cloned.1.call-start = ((), (), s32[]{:S(2)}) async-start(), calls=%async_computation.6 | async-start | bytes 327680 | tf_op jit(solution)/shard_map/while/body/eval_jaxpr/reduce_scatter | solution.py:135
  640.9 0.7 copy-start.2
  669.2 6.2 collective-permute-start.1
  675.4 48.7 %reduce-scatter.5.cloned.1.call-start = ((), (), s32[]{:S(2)}) async-start(), calls=%async_computation.6 | async-start | bytes 327680 | tf_op jit(solution)/shard_map/while/body/eval_jaxpr/reduce_scatter | solution.py:135
  704.4 0.7 copy-start.2
  731.8 6.2 collective-permute-start.1
  738.0 47.8 %reduce-scatter.5.cloned.1.call-start = ((), (), s32[]{:S(2)}) async-start(), calls=%async_computation.6 | async-start | bytes 327680 | tf_op jit(solution)/shard_map/while/body/eval_jaxpr/reduce_scatter | solution.py:135
  767.0 0.7 copy-start.2
  793.5 6.2 collective-permute-start.1
  799.6 111.1 %all-gather.5.cloned.1.call-start = ((), (), s32[]{:S(2)}) async-start(), calls=%async_computation.4 | async-start | bytes 12582912 | tf_op jit(solution)/shard_map/all_gather | solution.py:167
  800.2 214.6 %all-gather.3.cloned.1.call-start = ((), (), s32[]{:S(2)}) async-start(), calls=%async_computation.3 | async-start | bytes 12582912 | tf_op jit(solution)/shard_map/all_gather | solution.py:166
  804.4 24.9 %all-to-all-start = ((bf16[2,256,2,512]{3,1,0,2:T(8,128)(2,1)}), bf16[2,256,2,512]{3,1,0,2:T(8,128)(2,1)S(1)}, u32[]{:S(2)}, u32[]{:S(2)}) async-start(bf16[2,256,2,512]{3,1,0,2:T(8,128)(2,1)} %copy.10), calls=%async_computation.2 | async-start | bytes 2097152 | tf_op jit(solution)/shard_map/all_to_all | solution.py:164
Sparse Core Ops, SparseCore 0:
  35.9 18.6 reduce-scatter.2
  82.0 19.0 reduce-scatter.2
  128.5 19.9 reduce-scatter.2
  175.9 20.8 reduce-scatter.2
  209.7 35.3 reduce-scatter.2
  258.0 35.3 reduce-scatter.2
  306.3 35.3 reduce-scatter.2
  362.8 44.4 reduce-scatter.4
  427.5 43.2 reduce-scatter.4
  491.1 43.2 reduce-scatter.4
  578.2 19.6 reduce-scatter.4
  641.7 19.7 reduce-scatter.4
  705.2 18.7 reduce-scatter.4
  767.9 17.8 reduce-scatter.4
Sparse Core Ops, SparseCore 1:
  801.6 109.1 all-gather.4
  912.8 102.0 all-gather.2
where the time goes:
time: 1030 us
  waiting for transfers between devices  615 us (60%)
  matrix products  169 us (16%)
  blocking collectives  138 us (13%)
  starting transfers between devices  36.5 us (4%)
  other arithmetic  33.5 us (3%)
  local copies, waits for them, and re-layouts  23.8 us (2%)
  between operations  15.3 us (1%)
    reduce_scatter x7, waiting for transfers between devices, backward_turn(): lax.psum_scatter(norm_part, 'mp', scatter_dimension=1, tiled=True)  208 us
    reduce_scatter x7, waiting for transfers between devices, forward_turn(): branch_sum = lax.psum_scatter(branch, 'mp', scatter_dimension=1, tiled=True)  186 us
    all_gather x1, waiting for transfers between devices, shards(): pregrad_piece = lax.all_gather(pregrad_all, 'dp', axis=0, tiled=True)  93.5 us
    all_gather x1, waiting for transfers between devices, shards(): activated_piece = lax.all_gather(activated_all, 'dp', axis=0, tiled=True)  81.4 us
    dot_general x4, matrix products, backward_active(): lax.dot_general(gathered, weight_second, CONTRACT_LAST, preferred_element...  50.5 us
    ppermute x14, waiting for transfers between devices, shifted(): return lax.ppermute(shard, axis, pairs)  44.9 us
    dot_general x4, matrix products, backward_active(): lax.dot_general(pre_grad, weight_first, CONTRACT_LAST, preferred_element_...  43.8 us
    dot_general x4, matrix products, forward_active(): jnp.dot(normed, weight_first, preferred_element_type=jnp.float32)  41.4 us
  transfers between devices with their start and end apart: 31, of which 30 were waited for; matrix products, arithmetic and copies ran while one was open for 1% of the time, Pallas kernels for 0%

commit v1 on v0

--- a/solution.py
+++ b/solution.py
@@ -163,8 +163,13 @@
     packed = jnp.stack((normed_all, outgrad_all)).reshape(2, all_rows, replicas, half_width)
     swapped = lax.all_to_all(packed, "dp", split_axis=2, concat_axis=1, tiled=True)
     columns = swapped.reshape(2, replicas * all_rows, half_width)
-    pregrad_piece = lax.all_gather(pregrad_all, "dp", axis=0, tiled=True)
-    activated_piece = lax.all_gather(activated_all, "dp", axis=0, tiled=True)
+    pregrad_piece, activated_piece = jnp.split(
+        lax.all_gather(
+            jnp.concatenate([pregrad_all, activated_all], axis=1), "dp", axis=0, tiled=True
+        ),
+        [pregrad_all.shape[1]],
+        axis=1,
+    )
     normed_cols = columns[0]
     outgrad_cols = columns[1]
     in_term = lax.dot_general(

time: 1030 us -> 1040 us (level)
    all_gather x2 -> x1, waiting for transfers between devices: 175 us -> 176 us  [shards(): lax.all_gather(jnp.concatenate([pregrad_all, activated_all], axis=1), 'dp...]
  transfers between devices with their start and end apart: 31 -> 30, of which waited for: 30 -> 29; matrix products, arithmetic and copies ran while one was open for 1% -> 0% of each run, Pallas kernels for 0% -> 0%
where the time goes in v1:
time: 1040 us; the launch traced here: 1030 us
  waiting for transfers between devices  615 us (59%)
  matrix products  168 us (16%)
  blocking collectives  133 us (13%)
  other arithmetic  41.3 us (4%)
  starting transfers between devices  36.6 us (4%)
  local copies, waits for them, and re-layouts  23.8 us (2%)
  between operations  15.2 us (1%)
    reduce_scatter x7, waiting for transfers between devices, backward_turn(): lax.psum_scatter(norm_part, 'mp', scatter_dimension=1, tiled=True)  208 us
    reduce_scatter x7, waiting for transfers between devices, forward_turn(): branch_sum = lax.psum_scatter(branch, 'mp', scatter_dimension=1, tiled=True)  186 us
    all_gather x1, waiting for transfers between devices, shards(): lax.all_gather(jnp.concatenate([pregrad_all, activated_all], axis=1), 'dp...  176 us
    dot_general x4, matrix products, backward_active(): lax.dot_general(gathered, weight_second, CONTRACT_LAST, preferred_element...  50.5 us
    ppermute x14, waiting for transfers between devices, shifted(): return lax.ppermute(shard, axis, pairs)  44.9 us
    dot_general x4, matrix products, backward_active(): lax.dot_general(pre_grad, weight_first, CONTRACT_LAST, preferred_element_...  43.8 us
    dot_general x4, matrix products, forward_active(): jnp.dot(normed, weight_first, preferred_element_type=jnp.float32)  41.4 us
    psum x7, blocking collectives, backward_turn(): row_dot = lax.psum(jnp.sum(scaled * unit_own, axis=1), 'mp')  40.3 us
  transfers between devices with their start and end apart: 30, of which 29 were waited for; matrix products, arithmetic and copies ran while one was open for 0% of the time, Pallas kernels for 0%

profile of v1, /device:TPU:0, one launch (start us, length us, event | category | flops | bytes accessed | tf_op | source)
XLA Modules:
  0.0 1034.8 jit_solution(8562382189569789318)
XLA Ops:
  13.2 334.3 %while.42 = (s32[]{:T(128)}, bf16[64,256]{1,0:T(8,128)(2,1)S(1)}, bf16[4,64,1024]{2,1,0:T(8,128)(2,1)S(1)}, f32[4,64]{1,0:T(4,128)S(1)}, f32[4,64,8192]{2,1,0:T(...) while((s32[]{:T(128)}, bf16[64,256]{1,0:T(8,128)(2,1)S(1)}, ...), condition=%wide.region_5.6_spmd, body=%wide.region_0.5_spmd.sunk | while | flops 2152726528 | bytes 110303480 | solution.py:91
  14.0 6.5 all_gather.24
  20.5 14.5 %conditional.5 = (f32[64,1024]{1,0:T(8,128)S(1)}, bf16[4,64,1024]{2,1,0:T(8,128)(2,1)S(1)}, f32[4,64]{1,0:T(4,128)S(1)}, f32[4,64,8192]{2,1,0:T(8,128)}) conditional(s32[]{:T(128)} %convert_element_type.141, (bf16[4,64,1024]{2,1,0:T(8,128)(2,1)S(1)}, f32[4,64]{1,0:T(4,128)S(1)}, f32[4,64,8192]{2,1,0:T(8,128)}) %tuple.97, ...), branch_computations={%region_1.1_spmd, %region_2.3_spmd} | conditional | flops 2152660992 | bytes 107747168 | solution.py:74
  20.7 10.4 %bitcast_dynamic-update-slice_fusion = (f32[4,64,8192]{2,1,0:T(8,128)}, f32[64,8192]{1,0:T(8,128)S(1)}) fusion(f32[4,64,8192]{2,1,0:T(8,128)} %get-tuple-element.578, s32[]{:T(128)S(6)} %select_n.85, bf16[1024,8192]{1,0:T(8,128)(2,1)} %get-tuple-element.573, bf16[64,1024]{1,0:T(8,128)(2,1)S(1)} %get-tuple-element.571, f32[1024]{0:T(1024)S(1)} %bitcast.76, ...), kind=kOutput, calls=%fused_computation.6 | convolution fusion | flops 1074003968 | bytes 21106948 | tf_op jit(solution)/shard_map/while/body/eval_jaxpr/cond/branch_1_fun/dot_general | solution.py:57
  35.8 18.8 %reduce-scatter.3.cloned.1.call-done = f32[64,256]{1,0:T(8,128)} async-done(((f32[64,1024]{1,0:T(8,128)}), f32[64,256]{1,0:T(8,128)}) %reduce-scatter.3.cloned.1.call-update) | async-done | bytes 65552 | tf_op jit(solution)/shard_map/while/body/eval_jaxpr/reduce_scatter | solution.py:80
  61.1 5.4 all_gather.24
  66.5 14.5 %conditional.5 = (f32[64,1024]{1,0:T(8,128)S(1)}, bf16[4,64,1024]{2,1,0:T(8,128)(2,1)S(1)}, f32[4,64]{1,0:T(4,128)S(1)}, f32[4,64,8192]{2,1,0:T(8,128)}) conditional(s32[]{:T(128)} %convert_element_type.141, (bf16[4,64,1024]{2,1,0:T(8,128)(2,1)S(1)}, f32[4,64]{1,0:T(4,128)S(1)}, f32[4,64,8192]{2,1,0:T(8,128)}) %tuple.97, ...), branch_computations={%region_1.1_spmd, %region_2.3_spmd} | conditional | flops 2152660992 | bytes 107747168 | solution.py:74
  66.7 10.4 %bitcast_dynamic-update-slice_fusion = (f32[4,64,8192]{2,1,0:T(8,128)}, f32[64,8192]{1,0:T(8,128)S(1)}) fusion(f32[4,64,8192]{2,1,0:T(8,128)} %get-tuple-element.578, s32[]{:T(128)S(6)} %select_n.85, bf16[1024,8192]{1,0:T(8,128)(2,1)} %get-tuple-element.573, bf16[64,1024]{1,0:T(8,128)(2,1)S(1)} %get-tuple-element.571, f32[1024]{0:T(1024)S(1)} %bitcast.76, ...), kind=kOutput, calls=%fused_computation.6 | convolution fusion | flops 1074003968 | bytes 21106948 | tf_op jit(solution)/shard_map/while/body/eval_jaxpr/cond/branch_1_fun/dot_general | solution.py:57
  81.8 19.2 %reduce-scatter.3.cloned.1.call-done = f32[64,256]{1,0:T(8,128)} async-done(((f32[64,1024]{1,0:T(8,128)}), f32[64,256]{1,0:T(8,128)}) %reduce-scatter.3.cloned.1.call-update) | async-done | bytes 65552 | tf_op jit(solution)/shard_map/while/body/eval_jaxpr/reduce_scatter | solution.py:80
  107.6 5.4 all_gather.24
  113.0 14.5 %conditional.5 = (f32[64,1024]{1,0:T(8,128)S(1)}, bf16[4,64,1024]{2,1,0:T(8,128)(2,1)S(1)}, f32[4,64]{1,0:T(4,128)S(1)}, f32[4,64,8192]{2,1,0:T(8,128)}) conditional(s32[]{:T(128)} %convert_element_type.141, (bf16[4,64,1024]{2,1,0:T(8,128)(2,1)S(1)}, f32[4,64]{1,0:T(4,128)S(1)}, f32[4,64,8192]{2,1,0:T(8,128)}) %tuple.97, ...), branch_computations={%region_1.1_spmd, %region_2.3_spmd} | conditional | flops 2152660992 | bytes 107747168 | solution.py:74
  113.2 10.4 %bitcast_dynamic-update-slice_fusion = (f32[4,64,8192]{2,1,0:T(8,128)}, f32[64,8192]{1,0:T(8,128)S(1)}) fusion(f32[4,64,8192]{2,1,0:T(8,128)} %get-tuple-element.578, s32[]{:T(128)S(6)} %select_n.85, bf16[1024,8192]{1,0:T(8,128)(2,1)} %get-tuple-element.573, bf16[64,1024]{1,0:T(8,128)(2,1)S(1)} %get-tuple-element.571, f32[1024]{0:T(1024)S(1)} %bitcast.76, ...), kind=kOutput, calls=%fused_computation.6 | convolution fusion | flops 1074003968 | bytes 21106948 | tf_op jit(solution)/shard_map/while/body/eval_jaxpr/cond/branch_1_fun/dot_general | solution.py:57
  128.3 20.1 %reduce-scatter.3.cloned.1.call-done = f32[64,256]{1,0:T(8,128)} async-done(((f32[64,1024]{1,0:T(8,128)}), f32[64,256]{1,0:T(8,128)}) %reduce-scatter.3.cloned.1.call-update) | async-done | bytes 65552 | tf_op jit(solution)/shard_map/while/body/eval_jaxpr/reduce_scatter | solution.py:80
  155.0 5.4 all_gather.24
  160.4 14.5 %conditional.5 = (f32[64,1024]{1,0:T(8,128)S(1)}, bf16[4,64,1024]{2,1,0:T(8,128)(2,1)S(1)}, f32[4,64]{1,0:T(4,128)S(1)}, f32[4,64,8192]{2,1,0:T(8,128)}) conditional(s32[]{:T(128)} %convert_element_type.141, (bf16[4,64,1024]{2,1,0:T(8,128)(2,1)S(1)}, f32[4,64]{1,0:T(4,128)S(1)}, f32[4,64,8192]{2,1,0:T(8,128)}) %tuple.97, ...), branch_computations={%region_1.1_spmd, %region_2.3_spmd} | conditional | flops 2152660992 | bytes 107747168 | solution.py:74
  160.6 10.3 %bitcast_dynamic-update-slice_fusion = (f32[4,64,8192]{2,1,0:T(8,128)}, f32[64,8192]{1,0:T(8,128)S(1)}) fusion(f32[4,64,8192]{2,1,0:T(8,128)} %get-tuple-element.578, s32[]{:T(128)S(6)} %select_n.85, bf16[1024,8192]{1,0:T(8,128)(2,1)} %get-tuple-element.573, bf16[64,1024]{1,0:T(8,128)(2,1)S(1)} %get-tuple-element.571, f32[1024]{0:T(1024)S(1)} %bitcast.76, ...), kind=kOutput, calls=%fused_computation.6 | convolution fusion | flops 1074003968 | bytes 21106948 | tf_op jit(solution)/shard_map/while/body/eval_jaxpr/cond/branch_1_fun/dot_general | solution.py:57
  175.7 21.1 %reduce-scatter.3.cloned.1.call-done = f32[64,256]{1,0:T(8,128)} async-done(((f32[64,1024]{1,0:T(8,128)}), f32[64,256]{1,0:T(8,128)}) %reduce-scatter.3.cloned.1.call-update) | async-done | bytes 65552 | tf_op jit(solution)/shard_map/while/body/eval_jaxpr/reduce_scatter | solution.py:80
  203.3 5.4 all_gather.24
  209.5 35.6 %reduce-scatter.3.cloned.1.call-done = f32[64,256]{1,0:T(8,128)} async-done(((f32[64,1024]{1,0:T(8,128)}), f32[64,256]{1,0:T(8,128)}) %reduce-scatter.3.cloned.1.call-update) | async-done | bytes 65552 | tf_op jit(solution)/shard_map/while/body/eval_jaxpr/reduce_scatter | solution.py:80
  251.7 5.4 all_gather.24
  257.8 35.6 %reduce-scatter.3.cloned.1.call-done = f32[64,256]{1,0:T(8,128)} async-done(((f32[64,1024]{1,0:T(8,128)}), f32[64,256]{1,0:T(8,128)}) %reduce-scatter.3.cloned.1.call-update) | async-done | bytes 65552 | tf_op jit(solution)/shard_map/while/body/eval_jaxpr/reduce_scatter | solution.py:80
  300.0 5.4 all_gather.24
  306.1 35.6 %reduce-scatter.3.cloned.1.call-done = f32[64,256]{1,0:T(8,128)} async-done(((f32[64,1024]{1,0:T(8,128)}), f32[64,256]{1,0:T(8,128)}) %reduce-scatter.3.cloned.1.call-update) | async-done | bytes 65552 | tf_op jit(solution)/shard_map/while/body/eval_jaxpr/reduce_scatter | solution.py:80
  347.5 6.1 fusion.48
  356.2 443.2 %while.43 = (s32[]{:T(128)}, f32[64,256]{1,0:T(8,128)S(1)}, bf16[4,64,8192]{2,1,0:T(8,128)(2,1)}, bf16[4,64,1024]{2,1,0:T(8,128)(2,1)S(1)}, f32[256]{0:T(256)S(1...) while((s32[]{:T(128)}, f32[64,256]{1,0:T(8,128)S(1)}, ...), condition=%wide.region_13.14_spmd.clone, body=%wide.region_6.13_spmd.clone.sunk | while | flops 2157756928 | bytes 42672648 | solution.py:151
  356.3 5.4 all_gather.25
  362.5 44.6 %reduce-scatter.5.cloned.1.call-done = f32[64,256]{1,0:T(8,128)} async-done(((f32[64,1024]{1,0:T(8,128)}), f32[64,256]{1,0:T(8,128)}) %reduce-scatter.5.cloned.1.call-update) | async-done | bytes 65552 | tf_op jit(solution)/shard_map/while/body/eval_jaxpr/reduce_scatter | solution.py:135
  408.1 5.8 psum.23
  416.1 4.8 collective-permute-done.1
  420.9 5.4 all_gather.25
  427.2 43.4 %reduce-scatter.5.cloned.1.call-done = f32[64,256]{1,0:T(8,128)} async-done(((f32[64,1024]{1,0:T(8,128)}), f32[64,256]{1,0:T(8,128)}) %reduce-scatter.5.cloned.1.call-update) | async-done | bytes 65552 | tf_op jit(solution)/shard_map/while/body/eval_jaxpr/reduce_scatter | solution.py:135
  471.6 5.8 psum.23
  484.5 5.4 all_gather.25
  490.7 43.4 %reduce-scatter.5.cloned.1.call-done = f32[64,256]{1,0:T(8,128)} async-done(((f32[64,1024]{1,0:T(8,128)}), f32[64,256]{1,0:T(8,128)}) %reduce-scatter.5.cloned.1.call-update) | async-done | bytes 65552 | tf_op jit(solution)/shard_map/while/body/eval_jaxpr/reduce_scatter | solution.py:135
  535.2 5.8 psum.23
  548.0 5.4 all_gather.25
  553.5 23.6 %conditional.6 = (f32[64,1024]{1,0:T(8,128)S(1)}, bf16[4,64,8192]{2,1,0:T(8,128)(2,1)}, bf16[4,64,1024]{2,1,0:T(8,128)(2,1)S(1)}) conditional(s32[]{:T(128)} %convert_element_type.142, (bf16[4,64,8192]{2,1,0:T(8,128)(2,1)}, bf16[4,64,1024]{2,1,0:T(8,128)(2,1)S(1)}) %tuple.101, (bf16[64,1024]{1,0:T(8,128)(2,1)S(1)}, bf16[8192,1024]{1,0:T(8,128)(2,1)}, ...), branch_computations={%region_7.7_spmd, %region_8.8_spmd} | conditional | flops 2157445120 | bytes 39452740 | solution.py:126
  553.5 12.6 %bitcast_dynamic-update-slice_fusion.2 = (bf16[4,64,8192]{2,1,0:T(8,128)(2,1)}, bf16[64,8192]{1,0:T(8,128)(2,1)S(1)}) fusion(bf16[4,64,8192]{2,1,0:T(8,128)(2,1)} %get-tuple-element.602, s32[]{:T(128)S(6)} %select_n.88, f32[4,64,8192]{2,1,0:T(8,128)} %get-tuple-element.599, bf16[64,1024]{1,0:T(8,128)(2,1)S(1)} %get-tuple-element.597, ...), kind=kOutput, calls=%fused_computation.41 | convolution fusion | flops 1083703296 | bytes 21102596 | tf_op jit(solution)/shard_map/while/body/eval_jaxpr/cond/branch_1_fun/dot_general | solution.py:111
  566.1 10.9 %fusion.52 = f32[64,1024]{1,0:T(8,128)S(1)} fusion(bf16[64,8192]{1,0:T(8,128)(2,1)S(1)} %get-tuple-element.748, bf16[1024,8192]{1,0:T(8,128)(2,1)} %get-tuple-element.601), kind=kOutput, calls=%fused_computation.77 | convolution fusion | flops 1073741824 | bytes 18087936 | tf_op jit(solution)/shard_map/while/body/eval_jaxpr/cond/branch_1_fun/dot_general | solution.py:115
  577.8 19.8 %reduce-scatter.5.cloned.1.call-done = f32[64,256]{1,0:T(8,128)} async-done(((f32[64,1024]{1,0:T(8,128)}), f32[64,256]{1,0:T(8,128)}) %reduce-scatter.5.cloned.1.call-update) | async-done | bytes 65552 | tf_op jit(solution)/shard_map/while/body/eval_jaxpr/reduce_scatter | solution.py:135
  598.7 5.8 psum.23
  611.6 5.4 all_gather.25
  617.0 23.6 %conditional.6 = (f32[64,1024]{1,0:T(8,128)S(1)}, bf16[4,64,8192]{2,1,0:T(8,128)(2,1)}, bf16[4,64,1024]{2,1,0:T(8,128)(2,1)S(1)}) conditional(s32[]{:T(128)} %convert_element_type.142, (bf16[4,64,8192]{2,1,0:T(8,128)(2,1)}, bf16[4,64,1024]{2,1,0:T(8,128)(2,1)S(1)}) %tuple.101, (bf16[64,1024]{1,0:T(8,128)(2,1)S(1)}, bf16[8192,1024]{1,0:T(8,128)(2,1)}, ...), branch_computations={%region_7.7_spmd, %region_8.8_spmd} | conditional | flops 2157445120 | bytes 39452740 | solution.py:126
  617.0 12.6 %bitcast_dynamic-update-slice_fusion.2 = (bf16[4,64,8192]{2,1,0:T(8,128)(2,1)}, bf16[64,8192]{1,0:T(8,128)(2,1)S(1)}) fusion(bf16[4,64,8192]{2,1,0:T(8,128)(2,1)} %get-tuple-element.602, s32[]{:T(128)S(6)} %select_n.88, f32[4,64,8192]{2,1,0:T(8,128)} %get-tuple-element.599, bf16[64,1024]{1,0:T(8,128)(2,1)S(1)} %get-tuple-element.597, ...), kind=kOutput, calls=%fused_computation.41 | convolution fusion | flops 1083703296 | bytes 21102596 | tf_op jit(solution)/shard_map/while/body/eval_jaxpr/cond/branch_1_fun/dot_general | solution.py:111
  629.6 10.9 %fusion.52 = f32[64,1024]{1,0:T(8,128)S(1)} fusion(bf16[64,8192]{1,0:T(8,128)(2,1)S(1)} %get-tuple-element.748, bf16[1024,8192]{1,0:T(8,128)(2,1)} %get-tuple-element.601), kind=kOutput, calls=%fused_computation.77 | convolution fusion | flops 1073741824 | bytes 18087936 | tf_op jit(solution)/shard_map/while/body/eval_jaxpr/cond/branch_1_fun/dot_general | solution.py:115
  641.4 19.8 %reduce-scatter.5.cloned.1.call-done = f32[64,256]{1,0:T(8,128)} async-done(((f32[64,1024]{1,0:T(8,128)}), f32[64,256]{1,0:T(8,128)}) %reduce-scatter.5.cloned.1.call-update) | async-done | bytes 65552 | tf_op jit(solution)/shard_map/while/body/eval_jaxpr/reduce_scatter | solution.py:135
  662.2 5.8 psum.23
  675.1 5.4 all_gather.25
  680.5 23.6 %conditional.6 = (f32[64,1024]{1,0:T(8,128)S(1)}, bf16[4,64,8192]{2,1,0:T(8,128)(2,1)}, bf16[4,64,1024]{2,1,0:T(8,128)(2,1)S(1)}) conditional(s32[]{:T(128)} %convert_element_type.142, (bf16[4,64,8192]{2,1,0:T(8,128)(2,1)}, bf16[4,64,1024]{2,1,0:T(8,128)(2,1)S(1)}) %tuple.101, (bf16[64,1024]{1,0:T(8,128)(2,1)S(1)}, bf16[8192,1024]{1,0:T(8,128)(2,1)}, ...), branch_computations={%region_7.7_spmd, %region_8.8_spmd} | conditional | flops 2157445120 | bytes 39452740 | solution.py:126
  680.5 12.6 %bitcast_dynamic-update-slice_fusion.2 = (bf16[4,64,8192]{2,1,0:T(8,128)(2,1)}, bf16[64,8192]{1,0:T(8,128)(2,1)S(1)}) fusion(bf16[4,64,8192]{2,1,0:T(8,128)(2,1)} %get-tuple-element.602, s32[]{:T(128)S(6)} %select_n.88, f32[4,64,8192]{2,1,0:T(8,128)} %get-tuple-element.599, bf16[64,1024]{1,0:T(8,128)(2,1)S(1)} %get-tuple-element.597, ...), kind=kOutput, calls=%fused_computation.41 | convolution fusion | flops 1083703296 | bytes 21102596 | tf_op jit(solution)/shard_map/while/body/eval_jaxpr/cond/branch_1_fun/dot_general | solution.py:111
  693.2 11.0 %fusion.52 = f32[64,1024]{1,0:T(8,128)S(1)} fusion(bf16[64,8192]{1,0:T(8,128)(2,1)S(1)} %get-tuple-element.748, bf16[1024,8192]{1,0:T(8,128)(2,1)} %get-tuple-element.601), kind=kOutput, calls=%fused_computation.77 | convolution fusion | flops 1073741824 | bytes 18087936 | tf_op jit(solution)/shard_map/while/body/eval_jaxpr/cond/branch_1_fun/dot_general | solution.py:115
  704.9 18.9 %reduce-scatter.5.cloned.1.call-done = f32[64,256]{1,0:T(8,128)} async-done(((f32[64,1024]{1,0:T(8,128)}), f32[64,256]{1,0:T(8,128)}) %reduce-scatter.5.cloned.1.call-update) | async-done | bytes 65552 | tf_op jit(solution)/shard_map/while/body/eval_jaxpr/reduce_scatter | solution.py:135
  724.9 5.8 psum.23
  737.7 5.4 all_gather.25
  743.1 23.6 %conditional.6 = (f32[64,1024]{1,0:T(8,128)S(1)}, bf16[4,64,8192]{2,1,0:T(8,128)(2,1)}, bf16[4,64,1024]{2,1,0:T(8,128)(2,1)S(1)}) conditional(s32[]{:T(128)} %convert_element_type.142, (bf16[4,64,8192]{2,1,0:T(8,128)(2,1)}, bf16[4,64,1024]{2,1,0:T(8,128)(2,1)S(1)}) %tuple.101, (bf16[64,1024]{1,0:T(8,128)(2,1)S(1)}, bf16[8192,1024]{1,0:T(8,128)(2,1)}, ...), branch_computations={%region_7.7_spmd, %region_8.8_spmd} | conditional | flops 2157445120 | bytes 39452740 | solution.py:126
  743.1 12.6 %bitcast_dynamic-update-slice_fusion.2 = (bf16[4,64,8192]{2,1,0:T(8,128)(2,1)}, bf16[64,8192]{1,0:T(8,128)(2,1)S(1)}) fusion(bf16[4,64,8192]{2,1,0:T(8,128)(2,1)} %get-tuple-element.602, s32[]{:T(128)S(6)} %select_n.88, f32[4,64,8192]{2,1,0:T(8,128)} %get-tuple-element.599, bf16[64,1024]{1,0:T(8,128)(2,1)S(1)} %get-tuple-element.597, ...), kind=kOutput, calls=%fused_computation.41 | convolution fusion | flops 1083703296 | bytes 21102596 | tf_op jit(solution)/shard_map/while/body/eval_jaxpr/cond/branch_1_fun/dot_general | solution.py:111
  755.8 11.0 %fusion.52 = f32[64,1024]{1,0:T(8,128)S(1)} fusion(bf16[64,8192]{1,0:T(8,128)(2,1)S(1)} %get-tuple-element.748, bf16[1024,8192]{1,0:T(8,128)(2,1)} %get-tuple-element.601), kind=kOutput, calls=%fused_computation.77 | convolution fusion | flops 1073741824 | bytes 18087936 | tf_op jit(solution)/shard_map/while/body/eval_jaxpr/cond/branch_1_fun/dot_general | solution.py:115
  767.5 18.0 %reduce-scatter.5.cloned.1.call-done = f32[64,256]{1,0:T(8,128)} async-done(((f32[64,1024]{1,0:T(8,128)}), f32[64,256]{1,0:T(8,128)}) %reduce-scatter.5.cloned.1.call-update) | async-done | bytes 65552 | tf_op jit(solution)/shard_map/while/body/eval_jaxpr/reduce_scatter | solution.py:135
  786.6 5.8 psum.23
  799.4 7.7 pad_maximum_fusion
  814.7 16.3 %psum.20 = f32[1,256]{1,0:T(1,128)} all-reduce(f32[1,256]{1,0:T(1,128)S(1)} %bitcast.80), channel_id=1, replica_groups=mesh['dp'=2,'pipe'=4,'mp'=4] {'dp'}, use_global_device_ids=true, to_apply=%region_14.15 | all-reduce | flops 256 | bytes 2048 | tf_op jit(solution)/shard_map/psum | solution.py:186
  831.1 176.2 %all-gather.2.cloned.1.call-done = bf16[512,16384]{1,0:T(8,128)(2,1)} async-done(((bf16[256,16384]{1,0:T(8,128)(2,1)}), bf16[512,16384]{1,0:T(8,128)(2,1)}) %all-gather.2.cloned.1.call-update) | async-done | bytes 16777232 | tf_op jit(solution)/shard_map/all_gather | solution.py:167
  1007.3 10.2 fusion.43
  1017.5 10.2 fusion.42
  (207 shorter events, 140.5 us)
Async XLA Ops:
  8.0 5.2 copy-start.3
  13.2 41.4 %reduce-scatter.3.cloned.1.call-start = ((), (), s32[]{:S(2)}) async-start(), calls=%async_computation.4 | async-start | bytes 327680 | tf_op jit(solution)/shard_map/while/body/eval_jaxpr/reduce_scatter | solution.py:80
  20.7 11.3 %copy-start = (bf16[8192,1024]{1,0:T(8,128)(2,1)S(1)}, bf16[8192,1024]{1,0:T(8,128)(2,1)}, u32[]{:S(2)}) copy-start(bf16[8192,1024]{1,0:T(8,128)(2,1)} %get-tuple-element.574) | copy-start | bytes 50331652 | tf_op jit(solution)/shard_map/while/body/eval_jaxpr/cond
  35.0 0.7 copy-start.1
  55.4 5.0 collective-permute-start
  60.4 40.7 %reduce-scatter.3.cloned.1.call-start = ((), (), s32[]{:S(2)}) async-start(), calls=%async_computation.4 | async-start | bytes 327680 | tf_op jit(solution)/shard_map/while/body/eval_jaxpr/reduce_scatter | solution.py:80
  66.7 11.3 %copy-start = (bf16[8192,1024]{1,0:T(8,128)(2,1)S(1)}, bf16[8192,1024]{1,0:T(8,128)(2,1)}, u32[]{:S(2)}) copy-start(bf16[8192,1024]{1,0:T(8,128)(2,1)} %get-tuple-element.574) | copy-start | bytes 50331652 | tf_op jit(solution)/shard_map/while/body/eval_jaxpr/cond
  81.1 0.7 copy-start.1
  101.9 5.0 collective-permute-start
  106.9 41.6 %reduce-scatter.3.cloned.1.call-start = ((), (), s32[]{:S(2)}) async-start(), calls=%async_computation.4 | async-start | bytes 327680 | tf_op jit(solution)/shard_map/while/body/eval_jaxpr/reduce_scatter | solution.py:80
  113.2 11.3 %copy-start = (bf16[8192,1024]{1,0:T(8,128)(2,1)S(1)}, bf16[8192,1024]{1,0:T(8,128)(2,1)}, u32[]{:S(2)}) copy-start(bf16[8192,1024]{1,0:T(8,128)(2,1)} %get-tuple-element.574) | copy-start | bytes 50331652 | tf_op jit(solution)/shard_map/while/body/eval_jaxpr/cond
  127.6 0.7 copy-start.1
  149.3 4.9 collective-permute-start
  154.3 42.5 %reduce-scatter.3.cloned.1.call-start = ((), (), s32[]{:S(2)}) async-start(), calls=%async_computation.4 | async-start | bytes 327680 | tf_op jit(solution)/shard_map/while/body/eval_jaxpr/reduce_scatter | solution.py:80
  160.6 11.3 %copy-start = (bf16[8192,1024]{1,0:T(8,128)(2,1)S(1)}, bf16[8192,1024]{1,0:T(8,128)(2,1)}, u32[]{:S(2)}) copy-start(bf16[8192,1024]{1,0:T(8,128)(2,1)} %get-tuple-element.574) | copy-start | bytes 50331652 | tf_op jit(solution)/shard_map/while/body/eval_jaxpr/cond
  175.0 0.7 copy-start.1
  197.6 5.0 collective-permute-start
  202.6 42.5 %reduce-scatter.3.cloned.1.call-start = ((), (), s32[]{:S(2)}) async-start(), calls=%async_computation.4 | async-start | bytes 327680 | tf_op jit(solution)/shard_map/while/body/eval_jaxpr/reduce_scatter | solution.py:80
  208.8 0.7 copy-start.1
  245.9 5.0 collective-permute-start
  250.9 42.5 %reduce-scatter.3.cloned.1.call-start = ((), (), s32[]{:S(2)}) async-start(), calls=%async_computation.4 | async-start | bytes 327680 | tf_op jit(solution)/shard_map/while/body/eval_jaxpr/reduce_scatter | solution.py:80
  257.1 0.7 copy-start.1
  294.2 5.0 collective-permute-start
  299.2 42.5 %reduce-scatter.3.cloned.1.call-start = ((), (), s32[]{:S(2)}) async-start(), calls=%async_computation.4 | async-start | bytes 327680 | tf_op jit(solution)/shard_map/while/body/eval_jaxpr/reduce_scatter | solution.py:80
  305.4 0.7 copy-start.1
  342.5 5.0 collective-permute-start
  347.5 8.7 copy-start.4
  356.2 50.8 %reduce-scatter.5.cloned.1.call-start = ((), (), s32[]{:S(2)}) async-start(), calls=%async_computation.5 | async-start | bytes 327680 | tf_op jit(solution)/shard_map/while/body/eval_jaxpr/reduce_scatter | solution.py:135
  361.7 0.7 copy-start.2
  414.8 6.2 collective-permute-start.1
  420.9 49.7 %reduce-scatter.5.cloned.1.call-start = ((), (), s32[]{:S(2)}) async-start(), calls=%async_computation.5 | async-start | bytes 327680 | tf_op jit(solution)/shard_map/while/body/eval_jaxpr/reduce_scatter | solution.py:135
  426.4 0.7 copy-start.2
  478.3 6.2 collective-permute-start.1
  484.5 49.7 %reduce-scatter.5.cloned.1.call-start = ((), (), s32[]{:S(2)}) async-start(), calls=%async_computation.5 | async-start | bytes 327680 | tf_op jit(solution)/shard_map/while/body/eval_jaxpr/reduce_scatter | solution.py:135
  490.0 0.7 copy-start.2
  541.9 6.2 collective-permute-start.1
  548.0 49.7 %reduce-scatter.5.cloned.1.call-start = ((), (), s32[]{:S(2)}) async-start(), calls=%async_computation.5 | async-start | bytes 327680 | tf_op jit(solution)/shard_map/while/body/eval_jaxpr/reduce_scatter | solution.py:135
  577.1 0.7 copy-start.2
  605.4 6.2 collective-permute-start.1
  611.6 49.6 %reduce-scatter.5.cloned.1.call-start = ((), (), s32[]{:S(2)}) async-start(), calls=%async_computation.5 | async-start | bytes 327680 | tf_op jit(solution)/shard_map/while/body/eval_jaxpr/reduce_scatter | solution.py:135
  640.6 0.7 copy-start.2
  668.9 6.2 collective-permute-start.1
  675.1 48.7 %reduce-scatter.5.cloned.1.call-start = ((), (), s32[]{:S(2)}) async-start(), calls=%async_computation.5 | async-start | bytes 327680 | tf_op jit(solution)/shard_map/while/body/eval_jaxpr/reduce_scatter | solution.py:135
  704.1 0.7 copy-start.2
  731.6 6.2 collective-permute-start.1
  737.7 47.8 %reduce-scatter.5.cloned.1.call-start = ((), (), s32[]{:S(2)}) async-start(), calls=%async_computation.5 | async-start | bytes 327680 | tf_op jit(solution)/shard_map/while/body/eval_jaxpr/reduce_scatter | solution.py:135
  766.8 0.7 copy-start.2
  793.3 6.2 collective-permute-start.1
  799.4 207.9 %all-gather.2.cloned.1.call-start = ((), (), s32[]{:S(2)}) async-start(), calls=%async_computation.3 | async-start | bytes 25165824 | tf_op jit(solution)/shard_map/all_gather | solution.py:167
  810.8 20.2 %all-to-all-start = ((bf16[2,256,2,512]{3,1,0,2:T(8,128)(2,1)}), bf16[2,256,2,512]{3,1,0,2:T(8,128)(2,1)S(1)}, u32[]{:S(2)}, u32[]{:S(2)}) async-start(bf16[2,256,2,512]{3,1,0,2:T(8,128)(2,1)} %copy.10), calls=%async_computation.2 | async-start | bytes 2097152 | tf_op jit(solution)/shard_map/all_to_all | solution.py:164
Sparse Core Ops, SparseCore 0:
  35.9 18.6 reduce-scatter.2
  81.9 19.0 reduce-scatter.2
  128.4 19.9 reduce-scatter.2
  175.8 20.8 reduce-scatter.2
  209.6 35.3 reduce-scatter.2
  257.9 35.3 reduce-scatter.2
  306.3 35.3 reduce-scatter.2
  362.6 44.4 reduce-scatter.4
  427.2 43.2 reduce-scatter.4
  490.8 43.2 reduce-scatter.4
  577.9 19.7 reduce-scatter.4
  641.5 19.6 reduce-scatter.4
  705.0 18.7 reduce-scatter.4
  767.6 17.8 reduce-scatter.4
Sparse Core Ops, SparseCore 1:
  807.3 200.0 all-gather.1
